TPU v7x, 512 devices: a whole 4x8x8 slice. The times are simulated.
512 devices in a mesh: grp: 16 (over y, core), path: 32 (over z, x).
Axes of the slice: x: 4, y: 8, z: 8, core: 2. Of those that a mesh axis runs over, the one named last changes fastest.
Arguments:
- link_state: bfloat16 [16, 16384, 256], P('grp', 'path'), may hold values from -6 to 6
- path_state: bfloat16 [16, 4096, 256], P('grp', 'path'), may hold values from -6 to 6
- path_links: int32 [4096, 8], P('path'), may hold values from -1 to 16383, as said below
- w_path_in: bfloat16 [256, 768], replicated, may hold values from -0.375 to 0.375
- w_path_hid: bfloat16 [256, 768], replicated, may hold values from -0.375 to 0.375
- w_link_in: bfloat16 [256, 768], replicated, may hold values from -0.375 to 0.375
- w_link_hid: bfloat16 [256, 768], replicated, may hold values from -0.375 to 0.375
- cotangent: bfloat16 [16, 4096, 128], P('grp', 'path'), may hold values from -0.0234375 to 0.0234375
Outputs:
- link_next: bfloat16 [16, 16384, 256], P('grp', 'path')
- path_final: bfloat16 [16, 4096, 256], P('grp', 'path')
- read_grad: float32 [128, 256], P('path')
Inputs may be any that keep to these rules, and one draw needn't show every extreme that they name: `path_links`: entry -1 marks no hop; each path's live entries come first and number two or more. In the rows of one device, at most 32 live entries name links of the block of 512 link ids held by any one index of path, and some block takes exactly 32.
All inputs are finite; a program needn't handle non-finite values.
Results may differ from a plain program's by a relative error of at most 0.0035.
Values may be sent and summed in bfloat16 or wider, within the bound.
A program may use at most 64 MiB of HBM per device.

v0:
```python
import jax
import jax.numpy as jnp
from jax import lax
from jax.sharding import PartitionSpec as P


def gated_update(projected, carried, w_hidden):
    width = carried.shape[1]
    recur = jnp.dot(carried.astype(jnp.bfloat16), w_hidden, preferred_element_type=jnp.float32)
    reset = jax.nn.sigmoid(projected[:, :width] + recur[:, :width])
    update = jax.nn.sigmoid(projected[:, width : 2 * width] + recur[:, width : 2 * width])
    candidate = jnp.tanh(projected[:, 2 * width :] + reset * recur[:, 2 * width :])
    return (1.0 - update) * candidate + update * carried


def shards(
    link_state, path_state, path_links, w_path_in, w_path_hid, w_link_in, w_link_hid, cotangent
):
    bf16, f32 = (jnp.bfloat16, jnp.float32)
    own_links = link_state[0]
    link_dev, width = own_links.shape
    peer_count = lax.axis_size("path")
    path_count, hop_count = path_links.shape
    entries = path_count * hop_count
    capacity = entries // peer_count
    slots = peer_count * capacity
    flat_ids = path_links.reshape(-1)
    is_live = flat_ids >= 0
    owner_id = jnp.where(is_live, flat_ids // link_dev, peer_count)
    local_id = jnp.where(is_live, flat_ids % link_dev, 0)
    marks = (owner_id[:, None] == jnp.arange(peer_count)[None, :]).astype(bf16)
    order = jnp.arange(entries)
    earlier = (order[None, :] < order[:, None]).astype(bf16)
    before = jnp.dot(earlier, marks, preferred_element_type=f32)
    slot_id = jnp.sum(before * marks.astype(f32), axis=1).astype(jnp.int32)
    dest = jnp.where(is_live, owner_id * capacity + slot_id, -1)
    slot_ids = jnp.arange(slots)
    route = dest[None, :] == slot_ids[:, None]
    requests = jnp.sum(jnp.where(route, local_id[None, :] + 1, 0), axis=1) - 1
    received = lax.all_to_all(
        requests.reshape(peer_count, capacity), "path", split_axis=0, concat_axis=0, tiled=True
    ).reshape(-1)
    want = (received[:, None] == jnp.arange(link_dev)[None, :]).astype(bf16)
    served = jnp.dot(want, own_links, preferred_element_type=f32).astype(bf16)
    got = lax.all_to_all(
        served.reshape(peer_count, capacity, width), "path", split_axis=0, concat_axis=0, tiled=True
    ).reshape(slots, width)
    route_t = (dest[:, None] == slot_ids[None, :]).astype(bf16)
    fetched = jnp.dot(route_t, got, preferred_element_type=f32).astype(bf16)
    projected = jnp.dot(fetched, w_path_in, preferred_element_type=f32)
    projected = projected.reshape(path_count, hop_count, 3 * width)
    live_grid = is_live.reshape(path_count, hop_count)
    carried = path_state[0].astype(f32)
    messages = []
    for hop_index in range(hop_count):
        renewed = gated_update(projected[:, hop_index], carried, w_path_hid)
        carried = jnp.where(live_grid[:, hop_index, None], renewed, carried)
        messages.append(carried.astype(bf16))
    path_final = carried.astype(bf16)
    flat_messages = jnp.stack(messages, axis=1).reshape(-1, width)
    outgoing = jnp.dot(route.astype(bf16), flat_messages, preferred_element_type=f32).astype(bf16)
    incoming = lax.all_to_all(
        outgoing.reshape(peer_count, capacity, width),
        "path",
        split_axis=0,
        concat_axis=0,
        tiled=True,
    ).reshape(slots, width)
    link_sum = lax.dot_general(want, incoming, (((0,), (0,)), ((), ())), preferred_element_type=f32)
    link_proj = jnp.dot(link_sum.astype(bf16), w_link_in, preferred_element_type=f32)
    link_next = gated_update(link_proj, own_links.astype(f32), w_link_hid).astype(bf16)
    grad_term = lax.dot_general(
        cotangent[0], path_final, (((0,), (0,)), ((), ())), preferred_element_type=f32
    )
    part = lax.psum_scatter(grad_term, "path", scatter_dimension=0, tiled=True)
    read_grad = lax.psum(part, "grp")
    return (link_next[None], path_final[None], read_grad)


def solution(mesh):
    return jax.shard_map(
        shards,
        mesh=mesh,
        in_specs=(
            P("grp", "path", None),
            P("grp", "path", None),
            P("path", None),
            P(),
            P(),
            P(),
            P(),
            P("grp", "path", None),
        ),
        out_specs=(P("grp", "path", None), P("grp", "path", None), P("path", None)),
        check_vma=False,
    )
```

profile of v0, /device:TPU:2, one launch (start us, length us, event | category | flops | bytes accessed | tf_op | source)
XLA Modules:
  0.0 300.5 jit_solution(5889730820409296890)
XLA Ops:
  7.2 0.9 copy.42
  8.1 0.1 reshape.161
  8.2 0.5 fusion.13
  8.7 0.5 select_reduce_fusion
  9.3 0.1 sub.41
  9.3 21.8 %all_to_all.16 = s32[32,1,32]{2,1,0:T(1,128)S(1)} all-to-all(s32[32,1,32]{2,1,0:T(1,128)S(1)} %sub.41), channel_id=1, replica_groups=mesh['grp'=16,'path'=32] {'path'}, dimensions={0} | all-to-all | bytes 8192 | tf_op jit(solution)/shard_map/all_to_all | solution.py:40
  31.1 0.5 broadcast.189
  31.6 0.7 reduce.3
  32.3 0.1 eq.29
  32.4 2.3 fusion.7
  34.7 5.0 %all-to-all-start.1 = ((bf16[32,32,256]{2,1,0:T(8,128)(2,1)}), bf16[32,32,256]{2,1,0:T(8,128)(2,1)S(1)}, u32[]{:S(2)}, u32[]{:S(2)}) async-start(bf16[32,32,256]{2,1,0:T(8,128)(2,1)} %bitcast.2), calls=%async_computation.1 | async-start | bytes 1048576 | tf_op jit(solution)/shard_map/all_to_all | solution.py:45
  39.7 0.2 fusion.141
  39.9 15.5 %all-to-all-done.1 = bf16[32,32,256]{2,1,0:T(8,128)(2,1)S(1)} async-done(((bf16[32,32,256]{2,1,0:T(8,128)(2,1)}), bf16[32,32,256]{2,1,0:T(8,128)(2,1)S(1)}, u32[]{:S(2)}, u32[]{:S(2)}) %all-to-all-start.1) | async-done | bytes 524320 | tf_op jit(solution)/shard_map/all_to_all | solution.py:45
  55.4 3.5 %convolution_bitcast_fusion = f32[128,8,768]{2,1,0:T(8,128)} fusion(bf16[256,768]{1,0:T(8,128)(2,1)S(1)} %copy-done, bf16[1024,256]{1,0:T(8,128)(2,1)S(1)} %bitcast.96, s32[1024]{0:T(1024)S(1)} %add_select_fusion.2), kind=kOutput, calls=%fused_computation.12 | convolution fusion | flops 940834816 | bytes 4067328 | tf_op jit(solution)/shard_map/dot_general | solution.py:50
  58.9 13.3 %fusion.171 = (f32[128,1,768]{2,1,0:T(1,128)S(1)}, f32[128,1,768]{2,1,0:T(1,128)S(1)}, f32[128,1,768]{2,1,0:T(1,128)S(1)}, f32[128,1,768]{2,1,0:T(1,128)S(1)}, f...) fusion(f32[128,8,768]{2,1,0:T(8,128)} %convolution_bitcast_fusion), kind=kLoop, calls=%fused_computation.235 | loop fusion | bytes 6291456 | tf_op jit(solution)/shard_map/slice | solution.py:56
  72.2 0.1 copy_bitcast_fusion.6
  72.3 0.1 bitcast_dynamic-update-slice_fusion.7
  72.4 0.2 fusion.157
  72.6 0.1 bitcast_dynamic-update-slice_fusion.6
  72.7 0.2 fusion.155
  73.0 0.1 copy_bitcast_fusion.4
  73.0 0.1 bitcast_dynamic-update-slice_fusion.5
  73.1 0.2 fusion.153
  73.4 0.1 bitcast_dynamic-update-slice_fusion.4
  73.5 0.2 fusion.151
  73.7 0.1 copy_bitcast_fusion.2
  73.8 0.1 bitcast_dynamic-update-slice_fusion.3
  73.9 0.2 fusion.149
  74.1 0.1 bitcast_dynamic-update-slice_fusion.2
  74.2 0.2 fusion.147
  74.4 0.1 copy_bitcast_fusion
  74.5 0.1 bitcast_dynamic-update-slice_fusion.1
  74.6 0.2 fusion.145
  74.9 0.1 bitcast_dynamic-update-slice_fusion
  75.0 1.8 fusion.9
  76.8 5.6 %all-to-all-start.2 = ((bf16[32,32,256]{2,1,0:T(8,128)(2,1)}), bf16[32,32,256]{2,1,0:T(8,128)(2,1)S(1)}, u32[]{:S(2)}, u32[]{:S(2)}) async-start(bf16[32,32,256]{2,1,0:T(8,128)(2,1)} %bitcast.30), calls=%async_computation.2 | async-start | bytes 1048576 | tf_op jit(solution)/shard_map/all_to_all | solution.py:62
  82.4 0.0 all-reduce.3.cloned.1.call-start
  82.4 0.9 convolution_bitcast_fusion.1
  83.3 0.0 all-reduce.3.cloned.1.call-update
  83.3 0.4 fusion.32
  83.7 1.3 dynamic-slice
  85.6 154.7 %all-reduce.3.cloned.1.call-done = f32[128,256]{0,1:T(8,128)} async-done(((f32[128,256]{0,1:T(8,128)}), f32[128,256]{0,1:T(8,128)}) %all-reduce.3.cloned.1.call-update) | async-done | bytes 131088
  240.3 1.0 constant_dynamic-slice_fusion
  241.3 46.5 %psum.7 = f32[4,256]{0,1:T(8,128)S(1)} all-reduce(f32[4,256]{0,1:T(8,128)S(1)} %constant_dynamic-slice_fusion), channel_id=1, replica_groups=mesh['grp'=16,'path'=32] {'grp'}, use_global_device_ids=true, to_apply=%region_3.4 | all-reduce | flops 1024 | bytes 8192 | tf_op jit(solution)/shard_map/psum | solution.py:76
  287.8 0.7 copy.52
  288.5 0.8 copy-done.2
  289.3 2.4 fusion.11
  291.7 2.0 fusion.35
  (23 shorter events, 0.1 us)
Async XLA Ops:
  7.2 48.3 %copy-start = (bf16[256,768]{1,0:T(8,128)(2,1)S(1)}, bf16[256,768]{1,0:T(8,128)(2,1)}, u32[]{:S(2)}) copy-start(bf16[256,768]{1,0:T(8,128)(2,1)} %param.11) | copy-start | bytes 1179652
  7.2 32.5 %copy-start.8 = (s32[128,8]{0,1:T(8,128)S(1)}, s32[128,8]{0,1:T(8,128)}, u32[]{:S(2)}) copy-start(s32[128,8]{0,1:T(8,128)} %param.10) | copy-start | bytes 12292
  7.2 32.5 %copy-start.1 = (bf16[256,768]{1,0:T(8,128)(2,1)S(1)}, bf16[256,768]{1,0:T(8,128)(2,1)}, u32[]{:S(2)}) copy-start(bf16[256,768]{1,0:T(8,128)(2,1)} %param.12) | copy-start | bytes 1179652
  7.2 32.5 %copy-start.6 = (bf16[1,128,256]{2,1,0:T(8,128)(2,1)S(1)}, bf16[1,128,256]{2,1,0:T(8,128)(2,1)}, u32[]{:S(2)}) copy-start(bf16[1,128,256]{2,1,0:T(8,128)(2,1)} %param.9) | copy-start | bytes 196612
  34.7 20.8 %all-to-all-start.1 = ((bf16[32,32,256]{2,1,0:T(8,128)(2,1)}), bf16[32,32,256]{2,1,0:T(8,128)(2,1)S(1)}, u32[]{:S(2)}, u32[]{:S(2)}) async-start(bf16[32,32,256]{2,1,0:T(8,128)(2,1)} %bitcast.2), calls=%async_computation.1 | async-start | bytes 1048576 | tf_op jit(solution)/shard_map/all_to_all | solution.py:45
  74.6 7.8 %copy-start.7 = (bf16[1,128,128]{2,1,0:T(8,128)(2,1)S(1)}, bf16[1,128,128]{2,1,0:T(8,128)(2,1)}, u32[]{:S(2)}) copy-start(bf16[1,128,128]{2,1,0:T(8,128)(2,1)} %param.15) | copy-start | bytes 98308
  74.9 8.5 %copy-start.3 = (bf16[1,512,256]{2,1,0:T(8,128)(2,1)S(1)}, bf16[1,512,256]{2,1,0:T(8,128)(2,1)}, u32[]{:S(2)}) copy-start(bf16[1,512,256]{2,1,0:T(8,128)(2,1)} %param.8) | copy-start | bytes 786436
  74.9 8.5 %copy-start.4 = (bf16[256,768]{1,0:T(8,128)(2,1)S(1)}, bf16[256,768]{1,0:T(8,128)(2,1)}, u32[]{:S(2)}) copy-start(bf16[256,768]{1,0:T(8,128)(2,1)} %param.14) | copy-start | bytes 1179652
  75.0 8.3 %copy-start.5 = (bf16[128,256]{1,0:T(8,128)(2,1)}, bf16[128,256]{1,0:T(8,128)(2,1)S(1)}, u32[]{:S(2)}) copy-start(bf16[128,256]{1,0:T(8,128)(2,1)S(1)} %get-tuple-element.16) | copy-start | bytes 196612
  76.8 211.7 %all-to-all-start.2 = ((bf16[32,32,256]{2,1,0:T(8,128)(2,1)}), bf16[32,32,256]{2,1,0:T(8,128)(2,1)S(1)}, u32[]{:S(2)}, u32[]{:S(2)}) async-start(bf16[32,32,256]{2,1,0:T(8,128)(2,1)} %bitcast.30), calls=%async_computation.2 | async-start | bytes 1048576 | tf_op jit(solution)/shard_map/all_to_all | solution.py:62
  82.4 157.9 %all-reduce.3.cloned.1.call-start = ((), (), s32[]{:S(2)}) async-start(), calls=%async_computation.3 | async-start | bytes 262144
  288.5 0.8 copy-start.2
Sparse Core Ops, SparseCore 0:
  87.2 153.0 all-reduce.2
where the time goes:
time: 301 us
  waiting for transfers between devices  170 us (56%)
  blocking collectives  68.2 us (23%)
  local copies, waits for them, and re-layouts  18.9 us (6%)
  between operations  15 us (5%)
  matrix products  13.4 us (4%)
  starting transfers between devices  10.6 us (4%)
  other arithmetic  4.16 us (1%)
    unnamed x2, waiting for transfers between devices  155 us
    psum x1, blocking collectives, shards(): read_grad = lax.psum(part, 'grp')  46.5 us
    all_to_all x1, blocking collectives, shards(): lax.all_to_all(requests.reshape(peer_count, capacity), 'path', split_axis...  21.8 us
    all_to_all x1, waiting for transfers between devices, shards(): lax.all_to_all(served.reshape(peer_count, capacity, width), 'path', split...  15.5 us
    slice x1, local copies, waits for them, and re-layouts, shards(): renewed = gated_update(projected[:, hop_index], carried, w_path_hid)  13.3 us
  transfers between devices with their start and end apart: 3, of which 2 were waited for; matrix products, arithmetic and copies ran while one was open for 1% of the time, Pallas kernels for 0%

commit v1 on v0

--- a/solution.py
+++ b/solution.py
@@ -73,7 +73,8 @@
         cotangent[0], path_final, (((0,), (0,)), ((), ())), preferred_element_type=f32
     )
     part = lax.psum_scatter(grad_term, "path", scatter_dimension=0, tiled=True)
-    read_grad = lax.psum(part, "grp")
+    parts = lax.all_gather(part, "grp", axis=0, tiled=False)
+    read_grad = parts.sum(axis=0)
     return (link_next[None], path_final[None], read_grad)
 
 

time: 301 us -> 273 us (0.907)
  the two profiles are of different devices: /device:TPU:2 before, /device:TPU:1 now
where the time goes in v1:
time: 273 us
  waiting for transfers between devices  167 us (61%)
  blocking collectives  43.8 us (16%)
  local copies, waits for them, and re-layouts  18.3 us (7%)
  between operations  15 us (5%)
  matrix products  13.4 us (5%)
  starting transfers between devices  10.2 us (4%)
  other arithmetic  4.78 us (2%)
    unnamed x2, waiting for transfers between devices  153 us
    all_to_all x1, blocking collectives, shards(): lax.all_to_all(requests.reshape(peer_count, capacity), 'path', split_axis...  22.1 us
    all_gather x1, blocking collectives, shards(): parts = lax.all_gather(part, 'grp', axis=0, tiled=False)  21.7 us
    all_to_all x1, waiting for transfers between devices, shards(): lax.all_to_all(served.reshape(peer_count, capacity, width), 'path', split...  14.4 us
    slice x1, local copies, waits for them, and re-layouts, shards(): renewed = gated_update(projected[:, hop_index], carried, w_path_hid)  13.3 us
    all_to_all x1, starting transfers between devices, shards(): lax.all_to_all(outgoing.reshape(peer_count, capacity, width), 'path', spl...  6.3 us
  transfers between devices with their start and end apart: 3, of which 2 were waited for; matrix products, arithmetic and copies ran while one was open for 2% of the time, Pallas kernels for 0%

profile of v1, /device:TPU:1, one launch (start us, length us, event | category | flops | bytes accessed | tf_op | source)
XLA Modules:
  0.0 272.6 jit_solution(6424181043531358821)
XLA Ops:
  7.2 0.9 copy.42
  8.1 0.1 reshape.161
  8.2 0.5 fusion.13
  8.7 0.5 select_reduce_fusion
  9.3 0.1 sub.41
  9.3 22.1 %all_to_all.16 = s32[32,1,32]{2,1,0:T(1,128)S(1)} all-to-all(s32[32,1,32]{2,1,0:T(1,128)S(1)} %sub.41), channel_id=1, replica_groups=mesh['grp'=16,'path'=32] {'path'}, dimensions={0} | all-to-all | bytes 8192 | tf_op jit(solution)/shard_map/all_to_all | solution.py:40
  31.4 0.5 broadcast.189
  31.9 0.7 reduce.4
  32.6 0.1 eq.29
  32.7 2.3 fusion.7
  35.0 3.9 %all-to-all-start.1 = ((bf16[32,32,256]{2,1,0:T(8,128)(2,1)}), bf16[32,32,256]{2,1,0:T(8,128)(2,1)S(1)}, u32[]{:S(2)}, u32[]{:S(2)}) async-start(bf16[32,32,256]{2,1,0:T(8,128)(2,1)} %bitcast.2), calls=%async_computation.1 | async-start | bytes 1048576 | tf_op jit(solution)/shard_map/all_to_all | solution.py:45
  38.9 0.2 fusion.141
  39.2 14.4 %all-to-all-done.1 = bf16[32,32,256]{2,1,0:T(8,128)(2,1)S(1)} async-done(((bf16[32,32,256]{2,1,0:T(8,128)(2,1)}), bf16[32,32,256]{2,1,0:T(8,128)(2,1)S(1)}, u32[]{:S(2)}, u32[]{:S(2)}) %all-to-all-start.1) | async-done | bytes 524320 | tf_op jit(solution)/shard_map/all_to_all | solution.py:45
  53.5 3.5 %convolution_bitcast_fusion = f32[128,8,768]{2,1,0:T(8,128)} fusion(bf16[256,768]{1,0:T(8,128)(2,1)S(1)} %copy-done, bf16[1024,256]{1,0:T(8,128)(2,1)S(1)} %bitcast.98, s32[1024]{0:T(1024)S(1)} %add_select_fusion.2), kind=kOutput, calls=%fused_computation.12 | convolution fusion | flops 940834816 | bytes 4067328 | tf_op jit(solution)/shard_map/dot_general | solution.py:50
  57.0 13.3 %fusion.171 = (f32[128,1,768]{2,1,0:T(1,128)S(1)}, f32[128,1,768]{2,1,0:T(1,128)S(1)}, f32[128,1,768]{2,1,0:T(1,128)S(1)}, f32[128,1,768]{2,1,0:T(1,128)S(1)}, f...) fusion(f32[128,8,768]{2,1,0:T(8,128)} %convolution_bitcast_fusion), kind=kLoop, calls=%fused_computation.235 | loop fusion | bytes 6291456 | tf_op jit(solution)/shard_map/slice | solution.py:56
  70.3 0.1 copy_bitcast_fusion
  70.4 0.1 bitcast_dynamic-update-slice_fusion.7
  70.5 0.2 fusion.157
  70.7 0.1 bitcast_dynamic-update-slice_fusion.6
  70.8 0.2 fusion.155
  71.1 0.1 copy_bitcast_fusion.2
  71.1 0.1 bitcast_dynamic-update-slice_fusion.5
  71.2 0.2 fusion.153
  71.5 0.1 bitcast_dynamic-update-slice_fusion.4
  71.6 0.2 fusion.151
  71.8 0.1 copy_bitcast_fusion.4
  71.9 0.1 bitcast_dynamic-update-slice_fusion.3
  72.0 0.2 fusion.149
  72.2 0.1 bitcast_dynamic-update-slice_fusion.2
  72.3 0.2 fusion.147
  72.5 0.1 copy_bitcast_fusion.6
  72.6 0.1 bitcast_dynamic-update-slice_fusion.1
  72.7 0.2 fusion.145
  73.0 0.1 bitcast_dynamic-update-slice_fusion
  73.1 1.8 fusion.9
  74.9 6.3 %all-to-all-start.2 = ((bf16[32,32,256]{2,1,0:T(8,128)(2,1)}), bf16[32,32,256]{2,1,0:T(8,128)(2,1)S(1)}, u32[]{:S(2)}, u32[]{:S(2)}) async-start(bf16[32,32,256]{2,1,0:T(8,128)(2,1)} %bitcast.30), calls=%async_computation.2 | async-start | bytes 1048576 | tf_op jit(solution)/shard_map/all_to_all | solution.py:62
  81.2 0.0 all-reduce.3.cloned.1.call-start
  81.3 0.9 convolution_bitcast_fusion.1
  82.2 0.4 fusion.32
  82.5 1.3 dynamic-slice
  84.5 152.6 %all-reduce.3.cloned.1.call-done = f32[128,256]{0,1:T(8,128)} async-done(((f32[128,256]{0,1:T(8,128)}), f32[128,256]{0,1:T(8,128)}) %all-reduce.3.cloned.1.call-update) | async-done | bytes 131088
  237.1 1.0 dynamic-slice_bitcast_fusion
  238.1 0.1 copy.52
  238.2 21.7 %all-gather.1 = f32[16,4,256]{2,1,0:T(4,128)S(1)} all-gather(f32[1,4,256]{2,1,0:T(4,128)S(1)} %copy.52), channel_id=2, replica_groups=mesh['grp'=16,'path'=32] {'grp'}, dimensions={0}, use_global_device_ids=true | all-gather | bytes 69632 | tf_op jit(solution)/shard_map/all_gather | solution.py:76
  259.9 0.6 reduce_sum.29
  260.5 0.8 copy-done.2
  261.3 2.4 fusion.11
  263.7 2.0 fusion.35
  (24 shorter events, 0.1 us)
Async XLA Ops:
  7.2 46.4 %copy-start = (bf16[256,768]{1,0:T(8,128)(2,1)S(1)}, bf16[256,768]{1,0:T(8,128)(2,1)}, u32[]{:S(2)}) copy-start(bf16[256,768]{1,0:T(8,128)(2,1)} %param.11) | copy-start | bytes 1179652
  7.2 31.7 %copy-start.8 = (s32[128,8]{0,1:T(8,128)S(1)}, s32[128,8]{0,1:T(8,128)}, u32[]{:S(2)}) copy-start(s32[128,8]{0,1:T(8,128)} %param.10) | copy-start | bytes 12292
  7.2 31.7 %copy-start.1 = (bf16[256,768]{1,0:T(8,128)(2,1)S(1)}, bf16[256,768]{1,0:T(8,128)(2,1)}, u32[]{:S(2)}) copy-start(bf16[256,768]{1,0:T(8,128)(2,1)} %param.12) | copy-start | bytes 1179652
  7.2 31.7 %copy-start.6 = (bf16[1,128,256]{2,1,0:T(8,128)(2,1)S(1)}, bf16[1,128,256]{2,1,0:T(8,128)(2,1)}, u32[]{:S(2)}) copy-start(bf16[1,128,256]{2,1,0:T(8,128)(2,1)} %param.9) | copy-start | bytes 196612
  35.0 18.5 %all-to-all-start.1 = ((bf16[32,32,256]{2,1,0:T(8,128)(2,1)}), bf16[32,32,256]{2,1,0:T(8,128)(2,1)S(1)}, u32[]{:S(2)}, u32[]{:S(2)}) async-start(bf16[32,32,256]{2,1,0:T(8,128)(2,1)} %bitcast.2), calls=%async_computation.1 | async-start | bytes 1048576 | tf_op jit(solution)/shard_map/all_to_all | solution.py:45
  72.7 8.5 %copy-start.7 = (bf16[1,128,128]{2,1,0:T(8,128)(2,1)S(1)}, bf16[1,128,128]{2,1,0:T(8,128)(2,1)}, u32[]{:S(2)}) copy-start(bf16[1,128,128]{2,1,0:T(8,128)(2,1)} %param.15) | copy-start | bytes 98308
  73.0 9.2 %copy-start.3 = (bf16[1,512,256]{2,1,0:T(8,128)(2,1)S(1)}, bf16[1,512,256]{2,1,0:T(8,128)(2,1)}, u32[]{:S(2)}) copy-start(bf16[1,512,256]{2,1,0:T(8,128)(2,1)} %param.8) | copy-start | bytes 786436
  73.0 9.2 %copy-start.4 = (bf16[256,768]{1,0:T(8,128)(2,1)S(1)}, bf16[256,768]{1,0:T(8,128)(2,1)}, u32[]{:S(2)}) copy-start(bf16[256,768]{1,0:T(8,128)(2,1)} %param.14) | copy-start | bytes 1179652
  73.1 9.0 %copy-start.5 = (bf16[128,256]{1,0:T(8,128)(2,1)}, bf16[128,256]{1,0:T(8,128)(2,1)S(1)}, u32[]{:S(2)}) copy-start(bf16[128,256]{1,0:T(8,128)(2,1)S(1)} %get-tuple-element.10) | copy-start | bytes 196612
  74.9 185.6 %all-to-all-start.2 = ((bf16[32,32,256]{2,1,0:T(8,128)(2,1)}), bf16[32,32,256]{2,1,0:T(8,128)(2,1)S(1)}, u32[]{:S(2)}, u32[]{:S(2)}) async-start(bf16[32,32,256]{2,1,0:T(8,128)(2,1)} %bitcast.30), calls=%async_computation.2 | async-start | bytes 1048576 | tf_op jit(solution)/shard_map/all_to_all | solution.py:62
  81.2 155.9 %all-reduce.3.cloned.1.call-start = ((), (), s32[]{:S(2)}) async-start(), calls=%async_computation.3 | async-start | bytes 262144
  260.5 0.8 copy-start.2
Sparse Core Ops, SparseCore 0:
  86.1 150.9 all-reduce.2
